TPU v7x, 32 devices: a whole 2x2x4 slice. The times are simulated.
32 devices in a mesh: pair: 4 (over y, core), fold: 8 (over z, x).
Axes of the slice: x: 2, y: 2, z: 4, core: 2. Of those that a mesh axis runs over, the one named last changes fastest.
Arguments:
- amplitudes: bfloat16 [4, 80, 640, 640], P(None, 'pair', 'fold'), may hold values from -6 to 6
- cycle_block: bfloat16 [640, 80, 8, 640], P('fold', None, 'pair'), may hold values from -0.078125 to 0.078125
- occ_sizes: int32 [8], replicated, may hold values from 1 to 20, 80 in all
- vir_sizes: int32 [8], replicated, may hold values from 1 to 160, 640 in all
- window_i: int32 [4], replicated, may hold values from 0 to 79
- window_occ: int32 [8], replicated, may hold values from 0 to 79
Outputs:
- residual: bfloat16 [4, 640, 8, 640], P(None, 'fold', 'pair')
Inputs may be any that keep to these rules, and one draw needn't show every extreme that they name: `occ_sizes`: the entries sum to 80. `vir_sizes`: the entries sum to 640.
All inputs are finite; a program needn't handle non-finite values.
Results may differ from a plain program's by a relative error of at most 0.001.
Values may be sent and summed in bfloat16 or wider, within the bound.
A program may use at most 128 MiB of HBM per device.

v0:
```python
import jax
import jax.numpy as jnp
from jax import lax
from jax.sharding import PartitionSpec as P

FOLDS = 4


def irrep_labels(sizes, count):
    boundaries = jnp.cumsum(sizes)
    positions = jnp.arange(count, dtype=jnp.int32)
    return jnp.sum((positions[:, None] >= boundaries[None, :]).astype(jnp.int32), axis=1)


def label_lookup(orbitals, labels, count):
    matches = orbitals[:, None] == jnp.arange(count, dtype=jnp.int32)[None, :]
    return jnp.sum(jnp.where(matches, labels[None, :], 0), axis=1)


def body(n_pair, n_fold, amplitudes, cycle_block, occ_sizes, vir_sizes, window_i, window_occ):
    c_local, occ_total, j_local, vir_total = cycle_block.shape
    n_i, k_local, a_rows, _ = amplitudes.shape
    v_pack = vir_total // FOLDS
    k_pack = occ_total // FOLDS
    a_sub = a_rows // n_pair
    fold = lax.axis_index("fold")
    pair = lax.axis_index("pair")
    occ_labels = irrep_labels(occ_sizes, occ_total)
    vir_labels = irrep_labels(vir_sizes, vir_total)
    c_labels = lax.dynamic_slice_in_dim(vir_labels, fold * c_local, c_local)
    a_labels = lax.dynamic_slice_in_dim(vir_labels, fold * a_rows, a_rows)
    k_labels = lax.dynamic_slice_in_dim(occ_labels, pair * k_local, k_local)
    i_labels = label_lookup(window_i, occ_labels, occ_total)
    j_orbitals = lax.dynamic_slice_in_dim(window_occ, pair * j_local, j_local)
    j_labels = label_lookup(j_orbitals, occ_labels, occ_total)
    ika = i_labels[:, None, None] ^ k_labels[None, :, None] ^ a_labels[None, None, :]
    packed_c = 0
    for q in range(FOLDS):
        cut = slice(q * v_pack, (q + 1) * v_pack)
        keep = ika[..., None] == vir_labels[cut]
        packed_c = packed_c + jnp.where(keep, amplitudes[..., cut], 0)
    moved = lax.all_to_all(
        packed_c.reshape(n_i, k_local, n_pair, a_sub, v_pack),
        "pair",
        split_axis=2,
        concat_axis=1,
        tiled=True,
    ).reshape(n_i, FOLDS, k_pack, a_sub, v_pack)
    own_a = lax.dynamic_slice_in_dim(a_labels, pair * a_sub, a_sub)
    ia = i_labels[:, None] ^ own_a[None, :]
    pieces = []
    for q in range(FOLDS):
        iac = ia[..., None] ^ vir_labels[q * v_pack : (q + 1) * v_pack]
        total = 0
        for s in range(FOLDS):
            keep = iac[:, None] == occ_labels[s * k_pack : (s + 1) * k_pack][None, :, None, None]
            total = total + jnp.where(keep, moved[:, s], 0)
        pieces.append(total)
    packed_k = jnp.concatenate(pieces, axis=-1)
    packed_k = packed_k.reshape(n_i, k_pack, a_sub, n_fold, c_local).transpose(3, 0, 2, 1, 4)
    packed_k = packed_k.reshape(n_fold, n_i * a_sub, k_pack * c_local)
    relaid = lax.all_to_all(packed_k, "fold", split_axis=0, concat_axis=0, tiled=True)
    gathered = lax.all_gather(relaid, "pair", axis=0, tiled=False)
    ckj = c_labels[:, None, None] ^ occ_labels[None, :, None] ^ j_labels[None, None, :]
    packed_w = 0
    for q in range(FOLDS):
        cut = slice(q * v_pack, (q + 1) * v_pack)
        keep = ckj[..., None] == vir_labels[cut]
        packed_w = packed_w + jnp.where(keep, cycle_block[..., cut], 0)
    packed_w = packed_w.reshape(c_local, FOLDS, k_pack, j_local * v_pack).transpose(1, 2, 0, 3)
    packed_w = packed_w.reshape(FOLDS, k_pack * c_local, j_local * v_pack)
    row_a = vir_labels.reshape(n_fold, n_pair, a_sub).transpose(1, 0, 2)
    row_labels = (row_a[:, :, None, :] ^ i_labels[:, None]).reshape(n_pair, n_fold, n_i * a_sub)
    partial_sum = 0
    for s in range(FOLDS):
        col_labels = (
            occ_labels[s * k_pack : (s + 1) * k_pack][:, None] ^ c_labels[None, :]
        ).reshape(-1)
        lhs = jnp.where(row_labels[..., None] == col_labels, gathered, 0)
        partial_sum = partial_sum + jnp.einsum(
            "pfrx,xn->fprn", lhs, packed_w[s], preferred_element_type=jnp.float32
        )
    flat = partial_sum.reshape(-1, j_local * v_pack)
    own = lax.psum_scatter(flat, "fold", scatter_dimension=0, tiled=True)
    own = own.astype(jnp.bfloat16).reshape(n_pair, n_i, a_sub, j_local, v_pack)
    own = own.transpose(1, 0, 2, 3, 4).reshape(n_i, a_rows, j_local, v_pack)
    iaj = i_labels[:, None, None] ^ a_labels[None, :, None] ^ j_labels[None, None, :]
    keep = iaj[..., None] == vir_labels
    return jnp.where(keep, jnp.concatenate([own] * FOLDS, axis=-1), 0)


def solution(mesh):
    sizes = (mesh.shape["pair"], mesh.shape["fold"])
    placed = (P(None, "pair", "fold", None), P("fold", None, "pair", None), P(), P(), P(), P())

    def run(*args):
        return body(*sizes, *args)

    return jax.shard_map(
        run, mesh=mesh, in_specs=placed, out_specs=P(None, "fold", "pair", None), check_vma=False
    )
```

profile of v0, /device:TPU:0, one launch (start us, length us, event | category | flops | bytes accessed | tf_op | source)
XLA Modules:
  0.0 380.5 jit_solution(2479154911337334194)
XLA Ops:
  6.5 0.8 reduce-window.17
  7.4 0.1 convert_reduce_fusion
  7.7 0.8 reduce-window.16
  8.5 0.1 convert_reduce_fusion.1
  8.6 0.7 fusion.42
  9.3 0.8 select_reduce_fusion
  10.2 9.5 %fusion.21 = bf16[4,20,80,160]{3,2,1,0:T(8,128)(2,1)S(1)} fusion(bf16[4,20,80,640]{3,2,1,0:T(8,128)(2,1)} %param.6, s32[160]{0:T(256)S(1)} %get-tuple-element.22, s32[160]{0:T(256)S(1)} %get-tuple-element.23, s32[160]{0:T(256)S(1)} %get-tuple-element.24, s32[160]{0:T(256)S(1)} %get-tuple-element.21, s32[4,20,80]{2,1,0:T(8,128)S(1)} %broadcast_xor_fusion.6), kind=kLoop, calls=%fused_computation.35 | loop fusion | flops 11264000 | bytes 10268160 | tf_op jit(solution)/shard_map/add | solution.py:41
  19.8 2.5 copy.45
  22.3 2.9 copy.46
  25.2 4.3 %all-to-all-start = ((bf16[4,20,4,20,160]{4,0,3,1,2:T(4,128)(2,1)}), bf16[4,20,4,20,160]{4,0,3,1,2:T(4,128)(2,1)S(1)}, u32[]{:S(2)}, u32[]{:S(2)}) async-start(bf16[4,20,4,20,160]{4,0,3,1,2:T(4,128)(2,1)} %copy.46), calls=%async_computation | async-start | bytes 6553600 | tf_op jit(solution)/shard_map/all_to_all | solution.py:42
  29.5 0.6 xor.310
  30.1 0.6 xor.318
  30.7 0.6 xor.321
  31.3 0.6 xor.324
  31.9 0.1 copy.44
  32.0 1.5 broadcast_xor_fusion.5
  33.5 34.4 %all-to-all-done = bf16[4,20,4,20,160]{4,0,3,1,2:T(4,128)(2,1)S(1)} async-done(((bf16[4,20,4,20,160]{4,0,3,1,2:T(4,128)(2,1)}), bf16[4,20,4,20,160]{4,0,3,1,2:T(4,128)(2,1)S(1)}, u32[]{:S(2)}, u32[]{:S(2)}) %all-to-all-start) | async-done | bytes 2048032 | tf_op jit(solution)/shard_map/all_to_all | solution.py:42
  67.9 2.6 fusion.40
  70.5 3.0 squeeze.17
  73.5 2.5 squeeze.18
  76.0 2.5 squeeze.19
  78.5 2.5 squeeze.40
  81.0 16.6 %fusion.24 = (bf16[4,20,20,2,80]{4,3,0,2,1:T(2,128)(2,1)S(1)}, bf16[4,20,20,2,80]{4,3,0,2,1:T(2,128)(2,1)S(1)}, bf16[4,20,20,2,80]{4,3,0,2,1:T(2,128)(2,1)S(1)}, bf16[4,20,20,2,80]{4,3,0,2,1:T(2,128)(2,1)S(1)}) fusion(bf16[4,20,20,2,80]{4,3,0,2,1:T(2,128)(2,1)S(1)} %squeeze.40, s32[4,20,2,80]{3,2,0,1:T(2,128)S(1)} %get-tuple-element.17, ...), kind=kLoop, calls=%fused_computation.57 | loop fusion | flops 11264000 | bytes 4301120 | tf_op jit(solution)/shard_map/add | solution.py:57
  97.6 4.9 %maximum_bitcast_fusion = bf16[8,4,20,20,80]{4,0,1,2,3:T(8,128)(2,1)S(1)} fusion(bf16[4,20,20,2,80]{4,3,0,2,1:T(2,128)(2,1)S(1)} %get-tuple-element.10, bf16[4,20,20,2,80]{4,3,0,2,1:T(2,128)(2,1)S(1)} %get-tuple-element.11, bf16[4,20,20,2,80]{4,3,0,2,1:T(2,128)(2,1)S(1)} %get-tuple-element.12, bf16[4,20,20,2,80]{4,3,0,2,1:T(2,128)(2,1)S(1)} %get-tuple-element.9), kind=kLoop, calls=%fused_computation.36 | loop fusion | flops 8192000 | bytes 4096000 | tf_op jit(solution)/shard_map/transpose | solution.py:60
  102.5 4.1 %copy.47 = bf16[8,4,20,20,80]{4,3,2,1,0:T(8,128)(2,1)} copy(bf16[8,4,20,20,80]{4,0,1,2,3:T(8,128)(2,1)S(1)} %maximum_bitcast_fusion) | data formatting | bytes 4096000 | tf_op jit(solution)/shard_map/transpose | solution.py:60
  106.6 5.3 %reshape.385 = bf16[8,80,1600]{2,1,0:T(8,128)(2,1)S(1)} reshape(bf16[8,4,20,20,80]{4,3,2,1,0:T(8,128)(2,1)} %copy.47) | data formatting | bytes 4096000 | tf_op jit(solution)/shard_map/reshape | solution.py:61
  111.9 55.9 %all_to_all.20 = bf16[8,80,1600]{2,1,0:T(8,128)(2,1)} all-to-all(bf16[8,80,1600]{2,1,0:T(8,128)(2,1)S(1)} %reshape.385), channel_id=1, replica_groups=mesh['pair'=4,'fold'=8] {'fold'}, dimensions={0} | all-to-all | bytes 4096000 | tf_op jit(solution)/shard_map/all_to_all | solution.py:62
  167.9 0.1 reshape.382
  168.0 0.1 broadcast_xor_fusion.9
  168.3 0.2 fusion.34
  168.5 0.9 broadcast_xor_fusion
  169.5 56.1 %fusion.14 = bf16[80,80,2,160]{3,2,1,0:T(2,128)(2,1)} fusion(bf16[80,80,2,640]{3,2,1,0:T(2,128)(2,1)} %param.7, s32[160]{0:T(256)S(1)} %get-tuple-element.22, s32[80,80,2]{2,1,0:T(8,128)S(1)} %broadcast_xor_fusion, s32[160]{0:T(256)S(1)} %get-tuple-element.23, s32[160]{0:T(256)S(1)} %copy-done.2, s32[160]{0:T(256)S(1)} %get-tuple-element.21), kind=kLoop, calls=%fused_computation.22 | loop fusion | flops 22528000 | bytes 20533760 | tf_op jit(solution)/shard_map/add | solution.py:69
  225.6 15.1 %reshape.394 = bf16[80,4,20,320]{3,2,1,0:T(8,128)(2,1)} reshape(bf16[80,80,2,160]{3,2,1,0:T(2,128)(2,1)} %fusion.14) | data formatting | bytes 8192000 | tf_op jit(solution)/shard_map/reshape | solution.py:70
  240.7 6.7 %copy.64 = bf16[80,4,20,320]{3,0,2,1:T(8,128)(2,1)} copy(bf16[80,4,20,320]{3,2,1,0:T(8,128)(2,1)} %reshape.394) | data formatting | bytes 8192000 | tf_op jit(solution)/shard_map/reshape | solution.py:70
  247.5 0.1 xor.300
  247.6 0.1 xor.298
  248.0 4.3 %fusion.39 = (bf16[1,20,80,320]{3,2,1,0:T(8,128)(2,1)S(1)}, bf16[1,20,80,320]{3,2,1,0:T(8,128)(2,1)S(1)}, bf16[1,20,80,320]{3,2,1,0:T(8,128)(2,1)}, bf16[1,20,80,320]{3,2,1,0:T(8,128)(2,1)}) fusion(bf16[4,20,80,320]{3,2,1,0:T(8,128)(2,1)} %bitcast.46), kind=kLoop, calls=%fused_computation.94 | loop fusion | bytes 8192000 | tf_op jit(solution)/shard_map/slice | solution.py:81
  252.3 8.1 %fusion.1 = f32[320,4,8,80]{0,3,2,1:T(8,128)S(1)} fusion(bf16[1600,320,1,1]{1,0,3,2:T(8,128)(2,1)} %bitcast.55, bf16[4,8,80,1600]{3,2,1,0:T(8,128)(2,1)} %bitcast.58, s32[1600]{0:T(1024)S(1)} %xor.329, s32[4,8,80]{2,1,0:T(8,128)S(1)} %broadcast_xor_fusion.8), kind=kOutput, calls=%fused_computation.9 | convolution fusion | flops 2629632000 | bytes 12509440 | tf_op jit(solution)/shard_map/pfrx,xn->fprn/dot_general | solution.py:80
  260.4 7.1 %fusion = f32[320,4,8,80]{0,3,2,1:T(8,128)} fusion(bf16[1600,320,1,1]{1,0,3,2:T(8,128)(2,1)S(1)} %bitcast.54, bf16[4,8,80,1600]{3,2,1,0:T(8,128)(2,1)S(1)} %bitcast.59, s32[1600]{0:T(1024)S(1)} %xor.306, s32[4,8,80]{2,1,0:T(8,128)S(1)} %broadcast_xor_fusion.8), kind=kOutput, calls=%fused_computation.8 | convolution fusion | flops 2629632000 | bytes 12509440 | tf_op jit(solution)/shard_map/pfrx,xn->fprn/dot_general | solution.py:80
  267.6 7.0 %fusion.2 = f32[320,4,8,80]{0,3,2,1:T(8,128)} fusion(bf16[1600,320,1,1]{1,0,3,2:T(8,128)(2,1)S(1)} %bitcast.53, bf16[4,8,80,1600]{3,2,1,0:T(8,128)(2,1)S(1)} %bitcast.60, s32[1600]{0:T(1024)S(1)} %xor.332, s32[4,8,80]{2,1,0:T(8,128)S(1)} %broadcast_xor_fusion.8), kind=kOutput, calls=%fused_computation.10 | convolution fusion | flops 2629632000 | bytes 12509440 | tf_op jit(solution)/shard_map/pfrx,xn->fprn/dot_general | solution.py:80
  274.6 8.2 %add_bitcast_fusion = f32[8,4,80,320]{3,2,0,1:T(8,128)S(1)} fusion(f32[320,4,8,80]{0,3,2,1:T(8,128)} %fusion.2, f32[320,4,8,80]{0,3,2,1:T(8,128)} %fusion, f32[320,4,8,80]{0,3,2,1:T(8,128)S(1)} %fusion.1, bf16[1600,320,1,1]{1,0,3,2:T(8,128)(2,1)S(1)} %bitcast.52, bf16[4,8,80,1600]{3,2,1,0:T(8,128)(2,1)S(1)} %bitcast.61, s32[1600]{0:T(1024)S(1)} %xor.335, ...), kind=kOutput, calls=%fused_computation.32 | convolution fusion | flops 2632089600 | bytes 22339840 | tf_op jit(solution)/shard_map/pfrx,xn->fprn/dot_general | solution.py:80
  282.9 2.2 copy.52
  285.2 0.1 broadcast_xor_fusion.1
  285.3 82.2 %reduce-scatter.2.cloned.1.call-done = f32[320,320]{1,0:T(8,128)} async-done(((f32[2560,320]{1,0:T(8,128)}), f32[320,320]{1,0:T(8,128)}) %reduce-scatter.2.cloned.1.call-update) | async-done | bytes 409616 | tf_op jit(solution)/shard_map/reduce_scatter | solution.py:84
  367.5 1.1 convert_element_type.45
  368.6 0.1 reshape.387
  368.7 0.2 copy.53
  369.0 4.5 %compare_select_fusion.32 = bf16[4,80,2,640]{3,2,1,0:T(2,128)(2,1)} fusion(bf16[4,80,2,160]{3,2,1,0:T(2,128)(2,1)S(1)} %bitcast.50, s32[640]{0:T(1024)S(1)} %convert_reduce_fusion, s32[4,80,2]{2,1,0:T(8,128)S(1)} %broadcast_xor_fusion.1), kind=kLoop, calls=%fused_computation.53 | loop fusion | flops 4096000 | bytes 1029120 | tf_op jit(solution)/shard_map/jit(_where)/select_n | solution.py:89
  (51 shorter events, 1.1 us)
Async XLA Ops:
  7.5 22.6 %copy-start.1 = (s32[160]{0:T(256)}, s32[160]{0:T(256)S(1)}, u32[]{:S(2)}) copy-start(s32[160]{0:T(256)S(1)} %get-tuple-element.24) | copy-start | bytes 1924
  7.6 12.2 %copy-start.3 = (s32[80]{0:T(128)}, s32[80]{0:T(128)S(1)}, u32[]{:S(2)}) copy-start(s32[80]{0:T(128)S(1)} %dynamic_slice.15) | copy-start | bytes 964
  10.1 9.7 %copy-start.11 = (s32[4]{0:T(128)}, s32[4]{0:T(128)S(1)}, u32[]{:S(2)}) copy-start(s32[4]{0:T(128)S(1)} %select_reduce_fusion) | copy-start | bytes 52
  25.2 42.7 %all-to-all-start = ((bf16[4,20,4,20,160]{4,0,3,1,2:T(4,128)(2,1)}), bf16[4,20,4,20,160]{4,0,3,1,2:T(4,128)(2,1)S(1)}, u32[]{:S(2)}, u32[]{:S(2)}) async-start(bf16[4,20,4,20,160]{4,0,3,1,2:T(4,128)(2,1)} %copy.46), calls=%async_computation | async-start | bytes 6553600 | tf_op jit(solution)/shard_map/all_to_all | solution.py:42
  29.5 222.8 %all-gather.3.cloned.1.call-start = ((), (), s32[]{:S(2)}) async-start(), calls=%async_computation.4 | async-start | bytes 10649600 | tf_op jit(solution)/shard_map/all_gather | solution.py:63
  70.5 10.5 %copy-start.5 = (s32[20]{0:T(128)S(1)}, s32[20]{0:T(128)}, u32[]{:S(2)}) copy-start(s32[20]{0:T(128)} %get-tuple-element.29) | copy-start | bytes 244
  70.5 10.5 %copy-start.6 = (s32[20]{0:T(128)S(1)}, s32[20]{0:T(128)}, u32[]{:S(2)}) copy-start(s32[20]{0:T(128)} %get-tuple-element.30) | copy-start | bytes 244
  70.5 10.5 %copy-start.8 = (s32[20]{0:T(128)S(1)}, s32[20]{0:T(128)}, u32[]{:S(2)}) copy-start(s32[20]{0:T(128)} %get-tuple-element.31) | copy-start | bytes 244
  111.8 56.1 %copy-start.4 = (s32[80]{0:T(128)S(1)}, s32[80]{0:T(128)}, u32[]{:S(2)}) copy-start(s32[80]{0:T(128)} %copy-done.3) | copy-start | bytes 964
  111.9 56.1 %copy-start.7 = (s32[20]{0:T(128)S(1)}, s32[20]{0:T(128)}, u32[]{:S(2)}) copy-start(s32[20]{0:T(128)} %get-tuple-element.30) | copy-start | bytes 244
  111.9 56.1 %copy-start.9 = (s32[20]{0:T(128)S(1)}, s32[20]{0:T(128)}, u32[]{:S(2)}) copy-start(s32[20]{0:T(128)} %get-tuple-element.31) | copy-start | bytes 244
  111.9 56.1 %copy-start.10 = (s32[20]{0:T(128)S(1)}, s32[20]{0:T(128)}, u32[]{:S(2)}) copy-start(s32[20]{0:T(128)} %get-tuple-element.32) | copy-start | bytes 244
  111.9 56.3 %copy-start.14 = (s32[8]{0:T(128)S(1)}, s32[8]{0:T(128)}, u32[]{:S(2)}) copy-start(s32[8]{0:T(128)} %param.11) | copy-start | bytes 100
  111.9 57.6 %copy-start.2 = (s32[160]{0:T(256)S(1)}, s32[160]{0:T(256)}, u32[]{:S(2)}) copy-start(s32[160]{0:T(256)} %copy-done.1) | copy-start | bytes 1924
  167.8 199.7 %reduce-scatter.2.cloned.1.call-start = ((), (), s32[]{:S(2)}) async-start(), calls=%async_computation.3 | async-start | bytes 4423680 | tf_op jit(solution)/shard_map/reduce_scatter | solution.py:84
  240.7 6.7 %copy-start.12 = (s32[4]{0:T(128)S(1)}, s32[4]{0:T(128)}, u32[]{:S(2)}) copy-start(s32[4]{0:T(128)} %copy-done.11) | copy-start | bytes 52
  252.3 8.1 %copy-start = (bf16[1,20,80,320]{3,2,1,0:T(8,128)(2,1)S(1)}, bf16[1,20,80,320]{3,2,1,0:T(8,128)(2,1)}, u32[]{:S(2)}) copy-start(bf16[1,20,80,320]{3,2,1,0:T(8,128)(2,1)} %get-tuple-element.8) | copy-start | bytes 3072004
  252.3 8.1 %copy-start.13 = (bf16[32,80,1600]{2,1,0:T(8,128)(2,1)S(1)}, bf16[32,80,1600]{2,1,0:T(8,128)(2,1)}, u32[]{:S(2)}) copy-start(bf16[32,80,1600]{2,1,0:T(8,128)(2,1)} %all-gather.3.cloned.1.call-done) | copy-start | bytes 24576004
Sparse Core Ops, SparseCore 0:
  168.0 56.5 all-gather.2
  285.2 82.2 reduce-scatter.1
where the time goes:
time: 387 us; the launch traced here: 381 us
  waiting for transfers between devices  117 us (30%)
  other arithmetic  98.3 us (25%)
  local copies, waits for them, and re-layouts  60.8 us (16%)
  blocking collectives  55.9 us (14%)
  matrix products  30.5 us (8%)
  between operations  14 us (4%)
  starting transfers between devices  4.31 us (1%)
    reduce_scatter x1, waiting for transfers between devices, body(): own = lax.psum_scatter(flat, 'fold', scatter_dimension=0, tiled=True)  82.2 us
    add x1, other arithmetic, body(): packed_w = packed_w + jnp.where(keep, cycle_block[..., cut], 0)  56.1 us
    all_to_all x1, blocking collectives, body(): lax.all_to_all(packed_k, 'fold', split_axis=0, concat_axis=0, tiled=True)  55.9 us
    all_to_all x1, waiting for transfers between devices, body(): lax.all_to_all(packed_c.reshape(n_i, k_local, n_pair, a_sub, v_pack), 'pa...  34.4 us
    dot_general x4, matrix products, body(): jnp.einsum('pfrx,xn->fprn', lhs, packed_w[s], preferred_element_type=jnp....  30.5 us
    reshape x2, local copies, waits for them, and re-layouts, body(): packed_w.reshape(c_local, FOLDS, k_pack, j_local * v_pack)  21.9 us
    add x1, other arithmetic, body(): total = total + jnp.where(keep, moved[:, s], 0)  16.6 us
    squeeze x4, local copies, waits for them, and re-layouts, body(): total = total + jnp.where(keep, moved[:, s], 0)  10.5 us
  transfers between devices with their start and end apart: 3, of which 2 were waited for; matrix products, arithmetic and copies ran while one was open for 23% of the time, Pallas kernels for 0%

commit v1 on v0

--- a/solution.py
+++ b/solution.py
@@ -59,7 +59,15 @@
     packed_k = jnp.concatenate(pieces, axis=-1)
     packed_k = packed_k.reshape(n_i, k_pack, a_sub, n_fold, c_local).transpose(3, 0, 2, 1, 4)
     packed_k = packed_k.reshape(n_fold, n_i * a_sub, k_pack * c_local)
-    relaid = lax.all_to_all(packed_k, "fold", split_axis=0, concat_axis=0, tiled=True)
+    ways, here = (lax.axis_size("fold"), lax.axis_index("fold"))
+    width = packed_k.shape[0] // ways
+    turned = jnp.roll(packed_k, -here * width, axis=0)
+    got = [lax.slice_in_dim(turned, 0, width, axis=0)]
+    for far in range(1, ways):
+        sent = lax.slice_in_dim(turned, far * width, (far + 1) * width, axis=0)
+        got.append(lax.ppermute(sent, "fold", [(d, (d + far) % ways) for d in range(ways)]))
+    line = jnp.concatenate(got[::-1], axis=0)
+    relaid = jnp.roll(line, (here + 1) * got[0].shape[0], axis=0)
     gathered = lax.all_gather(relaid, "pair", axis=0, tiled=False)
     ckj = c_labels[:, None, None] ^ occ_labels[None, :, None] ^ j_labels[None, None, :]
     packed_w = 0

time: 387 us -> 389 us (level)
  blocking collectives: 55.9 us -> 0 us
  waiting for transfers between devices: 117 us -> 158 us
  starting transfers between devices: 4.31 us -> 13.1 us
  other arithmetic: 98.3 us -> 103 us
    all_to_all x1 -> x0, blocking collectives: 55.9 us -> none  [body(): lax.all_to_all(packed_k, 'fold', split_axis=0, concat_axis=0, tiled=True)]
    ppermute x0 -> x7, waiting for transfers between devices: none -> 40.1 us  [body(): lax.ppermute(sent, 'fold', [(d, (d + far) % ways) for d in range(ways)])]
    ppermute x0 -> x7, starting transfers between devices: none -> 8.77 us  [body(): lax.ppermute(sent, 'fold', [(d, (d + far) % ways) for d in range(ways)])]
    concatenate x0 -> x2, other arithmetic: none -> 4.75 us  [the longest x1 2.49 us: body(): turned = jnp.roll(packed_k, -here * width, axis=0)]
  transfers between devices with their start and end apart: 3 -> 10, of which waited for: 2 -> 7; matrix products, arithmetic and copies ran while one was open for 23% -> 24% of each run, Pallas kernels for 0% -> 0%
where the time goes in v1:
time: 389 us; the launch traced here: 383 us
  waiting for transfers between devices  158 us (41%)
  other arithmetic  103 us (26%)
  local copies, waits for them, and re-layouts  63.2 us (16%)
  matrix products  30.6 us (8%)
  between operations  14.3 us (4%)
  starting transfers between devices  13.1 us (3%)
    reduce_scatter x1, waiting for transfers between devices, body(): own = lax.psum_scatter(flat, 'fold', scatter_dimension=0, tiled=True)  84 us
    add x1, other arithmetic, body(): packed_w = packed_w + jnp.where(keep, cycle_block[..., cut], 0)  56.3 us
    ppermute x7, waiting for transfers between devices, body(): lax.ppermute(sent, 'fold', [(d, (d + far) % ways) for d in range(ways)])  40.1 us
    all_to_all x1, waiting for transfers between devices, body(): lax.all_to_all(packed_c.reshape(n_i, k_local, n_pair, a_sub, v_pack), 'pa...  34.2 us
    dot_general x4, matrix products, body(): jnp.einsum('pfrx,xn->fprn', lhs, packed_w[s], preferred_element_type=jnp....  30.6 us
    reshape x2, local copies, waits for them, and re-layouts, body(): packed_w.reshape(c_local, FOLDS, k_pack, j_local * v_pack)  21.9 us
    add x1, other arithmetic, body(): total = total + jnp.where(keep, moved[:, s], 0)  16.6 us
    add x1, other arithmetic, body(): packed_c = packed_c + jnp.where(keep, amplitudes[..., cut], 0)  9.53 us
  transfers between devices with their start and end apart: 10, of which 7 were waited for; matrix products, arithmetic and copies ran while one was open for 24% of the time, Pallas kernels for 0%

profile of v1, /device:TPU:0, one launch (start us, length us, event | category | flops | bytes accessed | tf_op | source)
XLA Modules:
  0.0 382.8 jit_solution(705772280742949971)
XLA Ops:
  6.5 0.8 reduce-window.17
  7.7 0.8 reduce-window.16
  8.6 0.7 fusion.45
  9.3 0.8 select_reduce_fusion
  10.3 9.5 %fusion.21 = bf16[4,20,80,160]{3,2,1,0:T(8,128)(2,1)S(1)} fusion(bf16[4,20,80,640]{3,2,1,0:T(8,128)(2,1)} %param.8, s32[160]{0:T(256)S(1)} %get-tuple-element.30, s32[160]{0:T(256)S(1)} %get-tuple-element.31, s32[160]{0:T(256)S(1)} %get-tuple-element.32, s32[160]{0:T(256)S(1)} %get-tuple-element.29, s32[4,20,80]{2,1,0:T(8,128)S(1)} %broadcast_xor_fusion.6), kind=kLoop, calls=%fused_computation.39 | loop fusion | flops 11264000 | bytes 10268160 | tf_op jit(solution)/shard_map/add | solution.py:41
  19.8 2.5 copy.45
  22.3 2.9 copy.46
  25.2 4.3 %all-to-all-start = ((bf16[4,20,4,20,160]{4,0,3,1,2:T(4,128)(2,1)}), bf16[4,20,4,20,160]{4,0,3,1,2:T(4,128)(2,1)S(1)}, u32[]{:S(2)}, u32[]{:S(2)}) async-start(bf16[4,20,4,20,160]{4,0,3,1,2:T(4,128)(2,1)} %copy.46), calls=%async_computation | async-start | bytes 6553600 | tf_op jit(solution)/shard_map/all_to_all | solution.py:42
  29.5 0.6 xor.310
  30.1 0.7 xor.318
  30.8 0.7 xor.321
  31.5 0.6 xor.324
  32.2 1.5 broadcast_xor_fusion.5
  33.7 34.2 %all-to-all-done = bf16[4,20,4,20,160]{4,0,3,1,2:T(4,128)(2,1)S(1)} async-done(((bf16[4,20,4,20,160]{4,0,3,1,2:T(4,128)(2,1)}), bf16[4,20,4,20,160]{4,0,3,1,2:T(4,128)(2,1)S(1)}, u32[]{:S(2)}, u32[]{:S(2)}) %all-to-all-start) | async-done | bytes 2048032 | tf_op jit(solution)/shard_map/all_to_all | solution.py:42
  67.9 2.6 fusion.42
  70.5 3.0 squeeze.17
  73.5 2.5 squeeze.18
  76.0 0.6 squeeze.19
  76.6 2.5 squeeze.40
  79.1 16.6 %fusion.26 = (bf16[4,20,20,2,80]{4,3,0,2,1:T(2,128)(2,1)S(1)}, bf16[4,20,20,2,80]{4,3,0,2,1:T(2,128)(2,1)S(1)}, bf16[4,20,20,2,80]{4,3,0,2,1:T(2,128)(2,1)S(1)}, bf16[4,20,20,2,80]{4,3,0,2,1:T(2,128)(2,1)S(1)}) fusion(bf16[4,20,20,2,80]{4,3,0,2,1:T(2,128)(2,1)S(1)} %squeeze.40, s32[4,20,2,80]{3,2,0,1:T(2,128)S(1)} %get-tuple-element.25, ...), kind=kLoop, calls=%fused_computation.63 | loop fusion | flops 11264000 | bytes 4301120 | tf_op jit(solution)/shard_map/add | solution.py:57
  95.7 4.9 %maximum_bitcast_fusion = bf16[8,4,20,20,80]{4,0,1,2,3:T(8,128)(2,1)S(1)} fusion(bf16[4,20,20,2,80]{4,3,0,2,1:T(2,128)(2,1)S(1)} %get-tuple-element.11, bf16[4,20,20,2,80]{4,3,0,2,1:T(2,128)(2,1)S(1)} %get-tuple-element.12, bf16[4,20,20,2,80]{4,3,0,2,1:T(2,128)(2,1)S(1)} %get-tuple-element.13, bf16[4,20,20,2,80]{4,3,0,2,1:T(2,128)(2,1)S(1)} %get-tuple-element.10), kind=kLoop, calls=%fused_computation.40 | loop fusion | flops 8192000 | bytes 4096000 | tf_op jit(solution)/shard_map/transpose | solution.py:60
  100.6 4.1 %copy.47 = bf16[8,4,20,20,80]{4,3,2,1,0:T(8,128)(2,1)} copy(bf16[8,4,20,20,80]{4,0,1,2,3:T(8,128)(2,1)S(1)} %maximum_bitcast_fusion) | data formatting | bytes 4096000 | tf_op jit(solution)/shard_map/transpose | solution.py:60
  104.7 6.3 %reshape.385 = bf16[8,80,1600]{2,1,0:T(8,128)(2,1)} reshape(bf16[8,4,20,20,80]{4,3,2,1,0:T(8,128)(2,1)} %copy.47) | data formatting | bytes 4096000 | tf_op jit(solution)/shard_map/reshape | solution.py:61
  111.0 2.5 fusion.23
  113.5 0.9 fusion.43
  114.4 5.3 %collective-permute-start = (bf16[1,80,1600]{2,1,0:T(8,128)(2,1)}, bf16[1,80,1600]{2,1,0:T(8,128)(2,1)}, u32[]{:S(2)}, u32[]{:S(2)}) collective-permute-start(bf16[1,80,1600]{2,1,0:T(8,128)(2,1)} %get-tuple-element.24), channel_id=1, source_target_pairs={{0,7},{1,0},{2,1},{3,2},{4,3},{5,4},{6,5},{7,6},{8,15},{9,8},{10,9... | collective-permute-start | bytes 768008 | tf_op jit(solution)/shard_map/ppermute | solution.py:68
  119.7 0.4 collective-permute-start.1
  120.1 3.0 collective-permute-start.3
  123.1 3.7 collective-permute-done
  126.9 1.0 constant_dynamic-update-slice_fusion.6
  127.9 4.7 %collective-permute-done.1 = bf16[1,80,1600]{2,1,0:T(8,128)(2,1)} collective-permute-done((bf16[1,80,1600]{2,1,0:T(8,128)(2,1)}, bf16[1,80,1600]{2,1,0:T(8,128)(2,1)}, u32[]{:S(2)}, u32[]{:S(2)}) %collective-permute-start.1) | collective-permute-done | bytes 256032 | tf_op jit(solution)/shard_map/ppermute | solution.py:68
  132.6 1.0 constant_dynamic-update-slice_fusion.5
  133.6 4.7 %collective-permute-done.2 = bf16[1,80,1600]{2,1,0:T(8,128)(2,1)S(1)} collective-permute-done((bf16[1,80,1600]{2,1,0:T(8,128)(2,1)S(1)}, bf16[1,80,1600]{2,1,0:T(8,128)(2,1)S(1)}, u32[]{:S(2)}, u32[]{:S(2)}) %collective-permute-start.2) | collective-permute-done | bytes 256032 | tf_op jit(solution)/shard_map/ppermute | solution.py:68
  138.3 26.8 %collective-permute-done.3 = bf16[1,80,1600]{2,1,0:T(8,128)(2,1)S(1)} collective-permute-done((bf16[1,80,1600]{2,1,0:T(8,128)(2,1)S(1)}, bf16[1,80,1600]{2,1,0:T(8,128)(2,1)S(1)}, u32[]{:S(2)}, u32[]{:S(2)}) %collective-permute-start.3) | collective-permute-done | bytes 256032 | tf_op jit(solution)/shard_map/ppermute | solution.py:68
  165.5 2.3 fusion.22
  168.5 0.9 broadcast_xor_fusion
  169.4 56.3 %fusion.14 = bf16[80,80,2,160]{3,2,1,0:T(2,128)(2,1)} fusion(bf16[80,80,2,640]{3,2,1,0:T(2,128)(2,1)} %param.9, s32[160]{0:T(256)S(1)} %get-tuple-element.30, s32[80,80,2]{2,1,0:T(8,128)S(1)} %broadcast_xor_fusion, s32[160]{0:T(256)S(1)} %get-tuple-element.31, s32[160]{0:T(256)S(1)} %copy-done.3, s32[160]{0:T(256)S(1)} %get-tuple-element.29), kind=kLoop, calls=%fused_computation.22 | loop fusion | flops 22528000 | bytes 20533760 | tf_op jit(solution)/shard_map/add | solution.py:77
  225.7 15.1 %reshape.394 = bf16[80,4,20,320]{3,2,1,0:T(8,128)(2,1)} reshape(bf16[80,80,2,160]{3,2,1,0:T(2,128)(2,1)} %fusion.14) | data formatting | bytes 8192000 | tf_op jit(solution)/shard_map/reshape | solution.py:78
  240.9 6.7 %copy.64 = bf16[80,4,20,320]{3,0,2,1:T(8,128)(2,1)} copy(bf16[80,4,20,320]{3,2,1,0:T(8,128)(2,1)} %reshape.394) | data formatting | bytes 8192000 | tf_op jit(solution)/shard_map/reshape | solution.py:78
  248.1 4.3 %fusion.41 = (bf16[1,20,80,320]{3,2,1,0:T(8,128)(2,1)S(1)}, bf16[1,20,80,320]{3,2,1,0:T(8,128)(2,1)S(1)}, bf16[1,20,80,320]{3,2,1,0:T(8,128)(2,1)}, bf16[1,20,80,320]{3,2,1,0:T(8,128)(2,1)}) fusion(bf16[4,20,80,320]{3,2,1,0:T(8,128)(2,1)} %bitcast.46), kind=kLoop, calls=%fused_computation.108 | loop fusion | bytes 8192000 | tf_op jit(solution)/shard_map/slice | solution.py:89
  252.5 8.2 %fusion.1 = f32[320,4,8,80]{0,3,2,1:T(8,128)S(1)} fusion(bf16[1600,320,1,1]{1,0,3,2:T(8,128)(2,1)} %bitcast.55, bf16[4,8,80,1600]{3,2,1,0:T(8,128)(2,1)} %bitcast.58, s32[1600]{0:T(1024)S(1)} %xor.329, s32[4,8,80]{2,1,0:T(8,128)S(1)} %broadcast_xor_fusion.8), kind=kOutput, calls=%fused_computation.9 | convolution fusion | flops 2629632000 | bytes 12509440 | tf_op jit(solution)/shard_map/pfrx,xn->fprn/dot_general | solution.py:88
  260.6 7.1 %fusion = f32[320,4,8,80]{0,3,2,1:T(8,128)} fusion(bf16[1600,320,1,1]{1,0,3,2:T(8,128)(2,1)S(1)} %bitcast.54, bf16[4,8,80,1600]{3,2,1,0:T(8,128)(2,1)S(1)} %bitcast.59, s32[1600]{0:T(1024)S(1)} %xor.306, s32[4,8,80]{2,1,0:T(8,128)S(1)} %broadcast_xor_fusion.8), kind=kOutput, calls=%fused_computation.8 | convolution fusion | flops 2629632000 | bytes 12509440 | tf_op jit(solution)/shard_map/pfrx,xn->fprn/dot_general | solution.py:88
  267.7 7.0 %fusion.2 = f32[320,4,8,80]{0,3,2,1:T(8,128)} fusion(bf16[1600,320,1,1]{1,0,3,2:T(8,128)(2,1)S(1)} %bitcast.53, bf16[4,8,80,1600]{3,2,1,0:T(8,128)(2,1)S(1)} %bitcast.60, s32[1600]{0:T(1024)S(1)} %xor.332, s32[4,8,80]{2,1,0:T(8,128)S(1)} %broadcast_xor_fusion.8), kind=kOutput, calls=%fused_computation.10 | convolution fusion | flops 2629632000 | bytes 12509440 | tf_op jit(solution)/shard_map/pfrx,xn->fprn/dot_general | solution.py:88
  274.8 8.3 %add_bitcast_fusion = f32[8,4,80,320]{3,2,0,1:T(8,128)S(1)} fusion(f32[320,4,8,80]{0,3,2,1:T(8,128)} %fusion.2, f32[320,4,8,80]{0,3,2,1:T(8,128)} %fusion, f32[320,4,8,80]{0,3,2,1:T(8,128)S(1)} %fusion.1, bf16[1600,320,1,1]{1,0,3,2:T(8,128)(2,1)S(1)} %bitcast.52, bf16[4,8,80,1600]{3,2,1,0:T(8,128)(2,1)S(1)} %bitcast.61, s32[1600]{0:T(1024)S(1)} %xor.335, ...), kind=kOutput, calls=%fused_computation.36 | convolution fusion | flops 2632089600 | bytes 22339840 | tf_op jit(solution)/shard_map/pfrx,xn->fprn/dot_general | solution.py:88
  283.1 2.2 copy.52
  285.5 84.0 %reduce-scatter.2.cloned.1.call-done = f32[320,320]{1,0:T(8,128)} async-done(((f32[2560,320]{1,0:T(8,128)}), f32[320,320]{1,0:T(8,128)}) %reduce-scatter.2.cloned.1.call-update) | async-done | bytes 409616 | tf_op jit(solution)/shard_map/reduce_scatter | solution.py:92
  369.5 1.1 convert_element_type.45
  371.0 4.5 %compare_select_fusion.32 = bf16[4,80,2,640]{3,2,1,0:T(2,128)(2,1)} fusion(bf16[4,80,2,160]{3,2,1,0:T(2,128)(2,1)S(1)} %bitcast.50, s32[640]{0:T(1024)S(1)} %convert_reduce_fusion, s32[4,80,2]{2,1,0:T(8,128)S(1)} %broadcast_xor_fusion.1), kind=kLoop, calls=%fused_computation.57 | loop fusion | flops 4096000 | bytes 1029120 | tf_op jit(solution)/shard_map/jit(_where)/select_n | solution.py:97
  (77 shorter events, 2.8 us)
Async XLA Ops:
  7.5 22.6 %copy-start.2 = (s32[160]{0:T(256)}, s32[160]{0:T(256)S(1)}, u32[]{:S(2)}) copy-start(s32[160]{0:T(256)S(1)} %get-tuple-element.32) | copy-start | bytes 1924
  7.6 12.2 %copy-start.4 = (s32[80]{0:T(128)}, s32[80]{0:T(128)S(1)}, u32[]{:S(2)}) copy-start(s32[80]{0:T(128)S(1)} %dynamic_slice.18) | copy-start | bytes 964
  10.1 9.7 %copy-start.12 = (s32[4]{0:T(128)}, s32[4]{0:T(128)S(1)}, u32[]{:S(2)}) copy-start(s32[4]{0:T(128)S(1)} %select_reduce_fusion) | copy-start | bytes 52
  25.2 42.7 %all-to-all-start = ((bf16[4,20,4,20,160]{4,0,3,1,2:T(4,128)(2,1)}), bf16[4,20,4,20,160]{4,0,3,1,2:T(4,128)(2,1)S(1)}, u32[]{:S(2)}, u32[]{:S(2)}) async-start(bf16[4,20,4,20,160]{4,0,3,1,2:T(4,128)(2,1)} %copy.46), calls=%async_computation | async-start | bytes 6553600 | tf_op jit(solution)/shard_map/all_to_all | solution.py:42
  29.5 223.0 %all-gather.3.cloned.1.call-start = ((), (), s32[]{:S(2)}) async-start(), calls=%async_computation.3 | async-start | bytes 10649600 | tf_op jit(solution)/shard_map/all_gather | solution.py:71
  70.5 5.5 %copy-start = (bf16[4,1,20,20,160]{4,0,3,2,1:T(4,128)(2,1)S(1)}, bf16[4,1,20,20,160]{4,0,3,2,1:T(4,128)(2,1)}, u32[]{:S(2)}) copy-start(bf16[4,1,20,20,160]{4,0,3,2,1:T(4,128)(2,1)} %get-tuple-element.16) | copy-start | bytes 1536004
  70.5 8.6 %copy-start.6 = (s32[20]{0:T(128)S(1)}, s32[20]{0:T(128)}, u32[]{:S(2)}) copy-start(s32[20]{0:T(128)} %get-tuple-element.37) | copy-start | bytes 244
  70.5 8.7 %copy-start.7 = (s32[20]{0:T(128)S(1)}, s32[20]{0:T(128)}, u32[]{:S(2)}) copy-start(s32[20]{0:T(128)} %get-tuple-element.38) | copy-start | bytes 244
  70.5 8.7 %copy-start.9 = (s32[20]{0:T(128)S(1)}, s32[20]{0:T(128)}, u32[]{:S(2)}) copy-start(s32[20]{0:T(128)} %get-tuple-element.39) | copy-start | bytes 244
  114.4 12.5 %collective-permute-start = (bf16[1,80,1600]{2,1,0:T(8,128)(2,1)}, bf16[1,80,1600]{2,1,0:T(8,128)(2,1)}, u32[]{:S(2)}, u32[]{:S(2)}) collective-permute-start(bf16[1,80,1600]{2,1,0:T(8,128)(2,1)} %get-tuple-element.24), channel_id=1, source_target_pairs={{0,7},{1,0},{2,1},{3,2},{4,3},{5,4},{6,5},{7,6},{8,15},{9,8},{10,9... | collective-permute-start | bytes 768008 | tf_op jit(solution)/shard_map/ppermute | solution.py:68
  119.7 12.9 %collective-permute-start.1 = (bf16[1,80,1600]{2,1,0:T(8,128)(2,1)}, bf16[1,80,1600]{2,1,0:T(8,128)(2,1)}, u32[]{:S(2)}, u32[]{:S(2)}) collective-permute-start(bf16[1,80,1600]{2,1,0:T(8,128)(2,1)} %get-tuple-element.23), channel_id=1, source_target_pairs={{0,6},{1,7},{2,0},{3,1},{4,2},{5,3},{6,4},{7,5},{8,14},{9,15},{10,... | collective-permute-start | bytes 768008 | tf_op jit(solution)/shard_map/ppermute | solution.py:68
  120.1 18.1 %collective-permute-start.2 = (bf16[1,80,1600]{2,1,0:T(8,128)(2,1)S(1)}, bf16[1,80,1600]{2,1,0:T(8,128)(2,1)S(1)}, u32[]{:S(2)}, u32[]{:S(2)}) collective-permute-start(bf16[1,80,1600]{2,1,0:T(8,128)(2,1)S(1)} %get-tuple-element.22), channel_id=1, source_target_pairs={{0,5},{1,6},{2,7},{3,0},{4,1},{5,2},{6,3},{7,4},{8,13},{9,14},{10,... | collective-permute-start | bytes 768008 | tf_op jit(solution)/shard_map/ppermute | solution.py:68
  120.1 44.9 %collective-permute-start.3 = (bf16[1,80,1600]{2,1,0:T(8,128)(2,1)S(1)}, bf16[1,80,1600]{2,1,0:T(8,128)(2,1)S(1)}, u32[]{:S(2)}, u32[]{:S(2)}) collective-permute-start(bf16[1,80,1600]{2,1,0:T(8,128)(2,1)S(1)} %get-tuple-element.21), channel_id=1, source_target_pairs={{0,4},{1,5},{2,6},{3,7},{4,0},{5,1},{6,2},{7,3},{8,12},{9,13},{10,... | collective-permute-start | bytes 768008 | tf_op jit(solution)/shard_map/ppermute | solution.py:68
  123.1 42.1 %collective-permute-start.4 = (bf16[1,80,1600]{2,1,0:T(8,128)(2,1)S(1)}, bf16[1,80,1600]{2,1,0:T(8,128)(2,1)S(1)}, u32[]{:S(2)}, u32[]{:S(2)}) collective-permute-start(bf16[1,80,1600]{2,1,0:T(8,128)(2,1)S(1)} %get-tuple-element.20), channel_id=1, source_target_pairs={{0,3},{1,4},{2,5},{3,6},{4,7},{5,0},{6,1},{7,2},{8,11},{9,12},{10,... | collective-permute-start | bytes 768008 | tf_op jit(solution)/shard_map/ppermute | solution.py:68
  126.9 38.4 %collective-permute-start.5 = (bf16[1,80,1600]{2,1,0:T(8,128)(2,1)S(1)}, bf16[1,80,1600]{2,1,0:T(8,128)(2,1)S(1)}, u32[]{:S(2)}, u32[]{:S(2)}) collective-permute-start(bf16[1,80,1600]{2,1,0:T(8,128)(2,1)S(1)} %get-tuple-element.19), channel_id=1, source_target_pairs={{0,2},{1,3},{2,4},{3,5},{4,6},{5,7},{6,0},{7,1},{8,10},{9,11},{10,... | collective-permute-start | bytes 768008 | tf_op jit(solution)/shard_map/ppermute | solution.py:68
  132.6 32.8 %collective-permute-start.6 = (bf16[1,80,1600]{2,1,0:T(8,128)(2,1)S(1)}, bf16[1,80,1600]{2,1,0:T(8,128)(2,1)S(1)}, u32[]{:S(2)}, u32[]{:S(2)}) collective-permute-start(bf16[1,80,1600]{2,1,0:T(8,128)(2,1)S(1)} %get-tuple-element.18), channel_id=1, source_target_pairs={{0,1},{1,2},{2,3},{3,4},{4,5},{5,6},{6,7},{7,0},{8,9},{9,10},{10,1... | collective-permute-start | bytes 768008 | tf_op jit(solution)/shard_map/ppermute | solution.py:68
  165.4 2.5 copy-start.5
  165.4 2.5 copy-start.8
  165.4 2.5 copy-start.10
  165.4 2.5 copy-start.11
  165.5 2.7 copy-start.15
  167.7 1.7 copy-start.3
  167.8 201.8 %reduce-scatter.2.cloned.1.call-start = ((), (), s32[]{:S(2)}) async-start(), calls=%async_computation.2 | async-start | bytes 4423680 | tf_op jit(solution)/shard_map/reduce_scatter | solution.py:92
  240.9 6.7 %copy-start.13 = (s32[4]{0:T(128)S(1)}, s32[4]{0:T(128)}, u32[]{:S(2)}) copy-start(s32[4]{0:T(128)} %copy-done.12) | copy-start | bytes 52
  252.4 8.2 %copy-start.1 = (bf16[1,20,80,320]{3,2,1,0:T(8,128)(2,1)S(1)}, bf16[1,20,80,320]{3,2,1,0:T(8,128)(2,1)}, u32[]{:S(2)}) copy-start(bf16[1,20,80,320]{3,2,1,0:T(8,128)(2,1)} %get-tuple-element.9) | copy-start | bytes 3072004
  252.5 8.2 %copy-start.14 = (bf16[32,80,1600]{2,1,0:T(8,128)(2,1)S(1)}, bf16[32,80,1600]{2,1,0:T(8,128)(2,1)}, u32[]{:S(2)}) copy-start(bf16[32,80,1600]{2,1,0:T(8,128)(2,1)} %all-gather.3.cloned.1.call-done) | copy-start | bytes 24576004
Sparse Core Ops, SparseCore 0:
  167.9 58.4 all-gather.2
  285.4 84.0 reduce-scatter.1
